TPU v7x, 32 devices: a whole 2x2x4 slice. The times are simulated.
32 devices in a mesh: px: 8 (over z, x), py: 4 (over y, core).
Axes of the slice: x: 2, y: 2, z: 4, core: 2. Of those that a mesh axis runs over, the one named last changes fastest.
Arguments:
- particles: float32 [32, 2, 2, 128, 128], P(('px', 'py')), may hold values from -11 to 11
- orientation: int32 [32], P(('px', 'py')), may hold values from 0 to 7
- wedge_index: int32 [32], P(('px', 'py')), may hold values from 0 to 3
- half_set: int32 [32], P(('px', 'py')), may hold values from 0 to 1
- shell_map: int32 [2, 256, 256], P(None, ('px', 'py')), may hold values from 0 to 31, as said below
Outputs:
- half_maps: float32 [2, 2, 2, 256, 256], P(None, None, None, ('px', 'py'))
- fsc: float32 [32], replicated
Inputs may be any that keep to these rules, and one draw needn't show every extreme that they name: `shell_map`: every shell number occurs in every draw.
All inputs are finite; a program needn't handle non-finite values.
Results may differ from a plain program's by a relative error of at most 0.0003.
Values sent between devices are 32-bit elements; how exact they have to be, the bound alone decides.
No kernel may reach another device: no remote copies, remote signals or barrier semaphores. Data moves between devices by JAX's collectives and lax.ppermute only.
A program may use at most 64 MiB of HBM per device.

v0:
```python
import math
import jax
import jax.numpy as jnp
from jax import lax
from jax.sharding import PartitionSpec as P

NSHELL = 32
wedge_rise = (1, 3, 2, 3)
wedge_run = (1, 2, 1, 1)
sign_first = (1.0, -1.0, -1.0, 1.0, 1.0, -1.0, -1.0, 1.0)
sign_second = (1.0, 1.0, -1.0, -1.0, -1.0, -1.0, 1.0, 1.0)
highest = lax.Precision.HIGHEST


def select(lookup, position):
    entries = jnp.array(lookup)
    return jnp.sum(jnp.where(jnp.arange(len(lookup)) == position, entries, jnp.zeros_like(entries)))


def angle_table(sources, targets, extent):
    phases = sources[:, None] * targets[None, :] % extent
    angles = phases.astype(jnp.float32) * (2.0 * math.pi / extent)
    factor = 1.0 / math.sqrt(extent)
    return (jnp.cos(angles) * factor, jnp.sin(angles) * factor)


def coverage(plane_abs, spectral_abs, wedge_id):
    rise_value = select(wedge_rise, wedge_id)
    run_value = select(wedge_run, wedge_id)
    return (plane_abs[:, None] * run_value <= spectral_abs[None, :] * rise_value).astype(
        jnp.float32
    )


def shards(particles, orientation, wedge_index, half_set, shell_map):
    planes = particles.shape[2]
    box_side = particles.shape[3]
    extent = shell_map.shape[2]
    own_rows = shell_map.shape[1]
    plane_abs = jnp.abs((jnp.arange(planes, dtype=jnp.int32) - planes // 2) * (extent // planes))
    spectral = jnp.arange(extent, dtype=jnp.int32)
    spectral_abs = jnp.minimum(spectral, extent - spectral)
    cos_fwd, sin_fwd = angle_table(
        jnp.arange(box_side, dtype=jnp.int32) - box_side // 2, spectral, extent
    )
    totals = jnp.zeros((2, 2, planes, extent, extent), jnp.float32)
    source = particles[0]
    turn_index = orientation[0]
    swapped = turn_index % 2 == 1
    source = jnp.where(turn_index >= 4, jnp.roll(jnp.flip(source, 1), 1, 1), source)
    source = jnp.where(swapped, jnp.swapaxes(source, 2, 3), source)
    sign_outer = select(sign_first, turn_index)
    sign_inner = select(sign_second, turn_index)
    along_cos = jnp.einsum("czab,bk->czak", source, cos_fwd, precision=highest)
    along_sin = jnp.einsum("czab,bk->czak", source, sin_fwd, precision=highest)
    partial_turn = jnp.stack(
        [along_cos[0] + sign_inner * along_sin[1], along_cos[1] - sign_inner * along_sin[0]]
    )
    outer_cos = jnp.einsum("czak,aj->czjk", partial_turn, cos_fwd, precision=highest)
    outer_sin = jnp.einsum("czak,aj->czjk", partial_turn, sin_fwd, precision=highest)
    spectrum = jnp.stack(
        [outer_cos[0] + sign_outer * outer_sin[1], outer_cos[1] - sign_outer * outer_sin[0]]
    )
    covered = coverage(plane_abs, spectral_abs, wedge_index[0])
    covered = jnp.where(swapped, covered[:, None, :], covered[:, :, None])
    half_id = half_set[0]
    current = lax.dynamic_index_in_dim(totals, half_id, 0, False)
    totals = lax.dynamic_update_index_in_dim(totals, current + spectrum * covered, half_id, 0)
    reduced = lax.psum_scatter(totals, ("px", "py"), scatter_dimension=3, tiled=True)
    half_hot = (half_set[:, None] == jnp.arange(2)).astype(jnp.float32)
    wedge_hot = (wedge_index[:, None] == jnp.arange(4)).astype(jnp.float32)
    parity_hot = (orientation[:, None] % 2 == jnp.arange(2)).astype(jnp.float32)
    local_counts = jnp.einsum("ph,pw,pq->hwq", half_hot, wedge_hot, parity_hot, precision=highest)
    class_totals = lax.psum(local_counts, ("px", "py"))
    row_abs = lax.dynamic_slice_in_dim(
        spectral_abs, lax.axis_index(("px", "py")) * own_rows, own_rows
    )
    row_cover = jnp.stack([coverage(plane_abs, row_abs, wedge_id) for wedge_id in range(4)])
    column_cover = jnp.stack([coverage(plane_abs, spectral_abs, wedge_id) for wedge_id in range(4)])
    by_rows = jnp.einsum("hw,wzt->hzt", class_totals[:, :, 0], row_cover, precision=highest)
    by_columns = jnp.einsum("hw,wzk->hzk", class_totals[:, :, 1], column_cover, precision=highest)
    cover = by_rows[:, :, :, None] + by_columns[:, :, None, :]
    average = reduced / jnp.maximum(cover, 1.0)[:, None]
    cross = average[0, 0] * average[1, 0] + average[0, 1] * average[1, 1]
    power_first = average[0, 0] * average[0, 0] + average[0, 1] * average[0, 1]
    power_second = average[1, 0] * average[1, 0] + average[1, 1] * average[1, 1]
    stacked = jnp.stack([cross, power_first, power_second]).reshape(3, -1)
    membership = (shell_map.reshape(-1)[:, None] == jnp.arange(NSHELL)).astype(jnp.float32)
    shell_part = jnp.dot(stacked, membership, precision=highest)
    shell_total = lax.psum(shell_part, ("px", "py"))
    fsc = shell_total[0] / (jnp.sqrt(shell_total[1] * shell_total[2]) + 1e-06)
    n_rows = lax.axis_size("px")
    n_columns = lax.axis_size("py")
    cos_y, sin_y = angle_table(spectral, spectral, extent)
    middle_cos = jnp.einsum("hcztk,kp->hczpt", average, cos_y, precision=highest)
    middle_sin = jnp.einsum("hcztk,kp->hczpt", average, sin_y, precision=highest)
    middle = jnp.stack(
        [middle_cos[:, 0] - middle_sin[:, 1], middle_sin[:, 0] + middle_cos[:, 1]], axis=1
    )
    arrived = lax.all_to_all(
        lax.all_to_all(middle, "px", split_axis=3, concat_axis=4, tiled=True),
        "py",
        split_axis=3,
        concat_axis=4,
        tiled=True,
    )
    x_slot = spectral // own_rows
    x_source = (x_slot % n_rows * n_columns + x_slot // n_rows) * own_rows + spectral % own_rows
    cos_x, sin_x = angle_table(x_source, spectral, extent)
    final_cos = jnp.einsum("hczym,mx->hczyx", arrived, cos_x, precision=highest)
    final_sin = jnp.einsum("hczym,mx->hczyx", arrived, sin_x, precision=highest)
    half_maps = jnp.stack(
        [final_cos[:, 0] - final_sin[:, 1], final_sin[:, 0] + final_cos[:, 1]], axis=1
    )
    return (half_maps, fsc)


def solution(mesh):
    placed = (
        P(("px", "py"), None, None, None, None),
        P(("px", "py")),
        P(("px", "py")),
        P(("px", "py")),
        P(None, ("px", "py"), None),
    )
    return jax.shard_map(
        shards,
        mesh=mesh,
        in_specs=placed,
        out_specs=(P(None, None, None, ("px", "py"), None), P()),
        check_vma=False,
    )
```

profile of v0, /device:TPU:0, one launch (start us, length us, event | category | flops | bytes accessed | tf_op | source)
XLA Modules:
  0.0 240.1 jit_solution(11886774212349079399)
XLA Ops:
  7.9 1.1 copy.50
  9.0 2.0 fusion.38
  11.0 2.0 fusion.42
  14.5 1.5 convolution_bitcast_fusion.1
  16.0 1.5 convolution_bitcast_fusion
  18.1 0.8 fusion.81
  21.2 1.6 fusion.4
  23.0 0.9 copy-done.1
  24.0 1.3 copy-done
  25.6 42.0 %psum.14 = f32[2,4,2]{1,0,2:T(2,128)S(1)} all-reduce(f32[2,4,2]{1,0,2:T(2,128)S(1)} %multiply_bitcast_fusion), channel_id=1, replica_groups=mesh['px'=8,'py'=4] {'px','py'}, use_global_device_ids=true, to_apply=%region_5.6 | all-reduce | flops 16 | bytes 128 | tf_op jit(solution)/shard_map/psum | solution.py:74
  70.9 1.9 broadcast_multiply_fusion.10
  76.5 89.9 %reduce-scatter.2.cloned.1.call-done = f32[2,2,2,8,256]{4,3,2,1,0:T(8,128)} async-done(((f32[2,2,2,256,256]{4,3,2,1,0:T(8,128)}), f32[2,2,2,8,256]{4,3,2,1,0:T(8,128)}) %reduce-scatter.2.cloned.1.call-update) | async-done | bytes 65552 | tf_op jit(solution)/shard_map/reduce_scatter | solution.py:69
  166.4 0.8 broadcast_divide_fusion
  167.3 1.3 convolution_bitcast_fusion.2
  168.6 1.3 convolution_bitcast_fusion.3
  170.7 2.2 reshape.771
  173.0 3.4 %all-to-all-start = ((f32[8,1,2048]{2,1,0:T(1,128)}), f32[8,1,2048]{2,1,0:T(1,128)S(1)}, u32[]{:S(2)}, u32[]{:S(2)}) async-start(f32[8,1,2048]{2,1,0:T(1,128)} %reshape.771), calls=%async_computation.1 | async-start | bytes 131072 | tf_op jit(solution)/shard_map/all_to_all | solution.py:101
  176.7 39.8 %psum.15 = f32[3,32]{1,0:T(4,128)S(1)} all-reduce(f32[3,32]{1,0:T(4,128)S(1)} %fusion.5), channel_id=1, replica_groups=mesh['px'=8,'py'=4] {'px','py'}, use_global_device_ids=true, to_apply=%region_22.23 | all-reduce | flops 96 | bytes 768 | tf_op jit(solution)/shard_map/psum | solution.py:90
  218.0 1.6 reshape.772
  221.1 3.5 %all-to-all-start.1 = ((f32[4,1,4096]{2,1,0:T(1,128)}), f32[4,1,4096]{2,1,0:T(1,128)S(1)}, u32[]{:S(2)}, u32[]{:S(2)}) async-start(f32[4,1,4096]{2,1,0:T(1,128)} %reshape.773), calls=%async_computation.2 | async-start | bytes 131072 | tf_op jit(solution)/shard_map/all_to_all | solution.py:100
  225.2 3.6 %all-to-all-done.1 = f32[4,1,4096]{2,1,0:T(1,128)S(1)} async-done(((f32[4,1,4096]{2,1,0:T(1,128)}), f32[4,1,4096]{2,1,0:T(1,128)S(1)}, u32[]{:S(2)}, u32[]{:S(2)}) %all-to-all-start.1) | async-done | bytes 65568 | tf_op jit(solution)/shard_map/all_to_all | solution.py:100
  228.8 0.9 reduce.1
  230.0 1.3 fusion.14
  231.3 1.3 fusion.16
  (74 shorter events, 16.1 us)
Async XLA Ops:
  7.2 5.9 %copy-start.3 = (f32[8]{0:T(128)S(1)}, f32[8]{0:T(128)}, u32[]{:S(2)}) copy-start(f32[8]{0:T(128)} %constant.153.clone) | copy-start | bytes 100
  7.2 5.9 %copy-start.4 = (f32[8]{0:T(128)S(1)}, f32[8]{0:T(128)}, u32[]{:S(2)}) copy-start(f32[8]{0:T(128)} %constant.154.clone) | copy-start | bytes 100
  7.2 159.2 %reduce-scatter.2.cloned.1.call-start = ((), (), s32[]{:S(2)}) async-start(), calls=%async_computation.3 | async-start | bytes 2162688 | tf_op jit(solution)/shard_map/reduce_scatter | solution.py:69
  13.8 4.3 %copy-start.5 = (s32[4]{0:T(128)S(1)}, s32[4]{0:T(128)}, u32[]{:S(2)}) copy-start(s32[4]{0:T(128)} %constant.155.clone) | copy-start | bytes 52
  13.8 4.3 %copy-start.6 = (s32[4]{0:T(128)S(1)}, s32[4]{0:T(128)}, u32[]{:S(2)}) copy-start(s32[4]{0:T(128)} %constant.156.clone) | copy-start | bytes 52
  22.8 1.0 copy-start.1
  23.9 52.5 %copy-start.2 = (s32[2,8,256]{2,1,0:T(8,128)S(1)}, s32[2,8,256]{2,1,0:T(8,128)}, u32[]{:S(2)}) copy-start(s32[2,8,256]{2,1,0:T(8,128)} %param.29) | copy-start | bytes 49156
  24.0 1.4 copy-start
  173.0 43.6 %all-to-all-start = ((f32[8,1,2048]{2,1,0:T(1,128)}), f32[8,1,2048]{2,1,0:T(1,128)S(1)}, u32[]{:S(2)}, u32[]{:S(2)}) async-start(f32[8,1,2048]{2,1,0:T(1,128)} %reshape.771), calls=%async_computation.1 | async-start | bytes 131072 | tf_op jit(solution)/shard_map/all_to_all | solution.py:101
  221.1 7.7 %all-to-all-start.1 = ((f32[4,1,4096]{2,1,0:T(1,128)}), f32[4,1,4096]{2,1,0:T(1,128)S(1)}, u32[]{:S(2)}, u32[]{:S(2)}) async-start(f32[4,1,4096]{2,1,0:T(1,128)} %reshape.773), calls=%async_computation.2 | async-start | bytes 131072 | tf_op jit(solution)/shard_map/all_to_all | solution.py:100
Sparse Core Ops, SparseCore 0:
  25.5 140.9 reduce-scatter.1
where the time goes:
time: 241 us; the launch traced here: 240 us
  waiting for transfers between devices  93.5 us (39%)
  blocking collectives  81.8 us (34%)
  other arithmetic  18 us (7%)
  between operations  16.4 us (7%)
  matrix products  12.8 us (5%)
  local copies, waits for them, and re-layouts  10.6 us (4%)
  starting transfers between devices  6.93 us (3%)
    reduce_scatter x1, waiting for transfers between devices, shards(): lax.psum_scatter(totals, ('px', 'py'), scatter_dimension=3, tiled=True)  89.9 us
    psum x1, blocking collectives, shards(): class_totals = lax.psum(local_counts, ('px', 'py'))  42 us
    psum x1, blocking collectives, shards(): shell_total = lax.psum(shell_part, ('px', 'py'))  39.8 us
    unnamed x22, local copies, waits for them, and re-layouts  7.03 us
    mul x7, other arithmetic, coverage(): spectral_abs[None, :] * rise_value  6 us
  transfers between devices with their start and end apart: 3, of which 2 were waited for; matrix products, arithmetic and copies ran while one was open for 4% of the time, Pallas kernels for 0%

commit v1 on v0

--- a/solution.py
+++ b/solution.py
@@ -87,7 +87,7 @@
     stacked = jnp.stack([cross, power_first, power_second]).reshape(3, -1)
     membership = (shell_map.reshape(-1)[:, None] == jnp.arange(NSHELL)).astype(jnp.float32)
     shell_part = jnp.dot(stacked, membership, precision=highest)
-    shell_total = lax.psum(shell_part, ("px", "py"))
+    shell_total = lax.psum(lax.psum(shell_part, "py"), "px")
     fsc = shell_total[0] / (jnp.sqrt(shell_total[1] * shell_total[2]) + 1e-06)
     n_rows = lax.axis_size("px")
     n_columns = lax.axis_size("py")

time: 241 us -> 228 us (0.946)
  blocking collectives: 81.8 us -> 69.7 us
    psum x1 -> x2, blocking collectives: 39.8 us -> 27.7 us  [shards(): shell_total = lax.psum(lax.psum(shell_part, 'py'), 'px')]
where the time goes in v1:
time: 228 us
  waiting for transfers between devices  93.5 us (41%)
  blocking collectives  69.7 us (31%)
  other arithmetic  18 us (8%)
  between operations  16.4 us (7%)
  matrix products  12.8 us (6%)
  local copies, waits for them, and re-layouts  10.6 us (5%)
  starting transfers between devices  6.67 us (3%)
    reduce_scatter x1, waiting for transfers between devices, shards(): lax.psum_scatter(totals, ('px', 'py'), scatter_dimension=3, tiled=True)  89.9 us
    psum x1, blocking collectives, shards(): class_totals = lax.psum(local_counts, ('px', 'py'))  42 us
    psum x2, blocking collectives, shards(): shell_total = lax.psum(lax.psum(shell_part, 'py'), 'px')  27.7 us
    unnamed x22, local copies, waits for them, and re-layouts  7.03 us
    mul x7, other arithmetic, coverage(): spectral_abs[None, :] * rise_value  6 us
  transfers between devices with their start and end apart: 3, of which 2 were waited for; matrix products, arithmetic and copies ran while one was open for 4% of the time, Pallas kernels for 0%

profile of v1, /device:TPU:0, one launch (start us, length us, event | category | flops | bytes accessed | tf_op | source)
XLA Modules:
  0.0 227.7 jit_solution(15744842792918333681)
XLA Ops:
  7.9 1.1 copy.50
  9.0 2.0 fusion.38
  11.0 2.0 fusion.42
  14.5 1.5 convolution_bitcast_fusion.1
  16.0 1.5 convolution_bitcast_fusion
  21.2 1.6 fusion.4
  23.0 0.9 copy-done.1
  24.0 1.3 copy-done
  25.6 42.0 %psum.21 = f32[2,4,2]{1,0,2:T(2,128)S(1)} all-reduce(f32[2,4,2]{1,0,2:T(2,128)S(1)} %multiply_bitcast_fusion), channel_id=1, replica_groups=mesh['px'=8,'py'=4] {'px','py'}, use_global_device_ids=true, to_apply=%region_5.6 | all-reduce | flops 16 | bytes 128 | tf_op jit(solution)/shard_map/psum | solution.py:74
  70.9 1.9 broadcast_multiply_fusion.10
  76.5 89.9 %reduce-scatter.2.cloned.1.call-done = f32[2,2,2,8,256]{4,3,2,1,0:T(8,128)} async-done(((f32[2,2,2,256,256]{4,3,2,1,0:T(8,128)}), f32[2,2,2,8,256]{4,3,2,1,0:T(8,128)}) %reduce-scatter.2.cloned.1.call-update) | async-done | bytes 65552 | tf_op jit(solution)/shard_map/reduce_scatter | solution.py:69
  166.4 0.8 broadcast_divide_fusion
  167.3 1.3 convolution_bitcast_fusion.2
  168.6 1.3 convolution_bitcast_fusion.3
  170.7 2.2 reshape.771
  173.0 3.4 %all-to-all-start = ((f32[8,1,2048]{2,1,0:T(1,128)}), f32[8,1,2048]{2,1,0:T(1,128)S(1)}, u32[]{:S(2)}, u32[]{:S(2)}) async-start(f32[8,1,2048]{2,1,0:T(1,128)} %reshape.771), calls=%async_computation.1 | async-start | bytes 131072 | tf_op jit(solution)/shard_map/all_to_all | solution.py:101
  176.7 5.8 %psum.22 = f32[3,32]{1,0:T(4,128)S(1)} all-reduce(f32[3,32]{1,0:T(4,128)S(1)} %fusion.5), channel_id=1, replica_groups=mesh['px'=8,'py'=4] {'py'}, use_global_device_ids=true, to_apply=%region_22.23 | all-reduce | flops 96 | bytes 768 | tf_op jit(solution)/shard_map/psum | solution.py:90
  182.5 21.9 %psum.23 = f32[3,32]{1,0:T(4,128)S(1)} all-reduce(f32[3,32]{1,0:T(4,128)S(1)} %psum.22), channel_id=1, replica_groups=mesh['px'=8,'py'=4] {'px'}, use_global_device_ids=true, to_apply=%region_23.24 | all-reduce | flops 96 | bytes 768 | tf_op jit(solution)/shard_map/psum | solution.py:90
  205.8 1.6 reshape.772
  209.0 3.3 %all-to-all-start.1 = ((f32[4,1,4096]{2,1,0:T(1,128)}), f32[4,1,4096]{2,1,0:T(1,128)S(1)}, u32[]{:S(2)}, u32[]{:S(2)}) async-start(f32[4,1,4096]{2,1,0:T(1,128)} %reshape.773), calls=%async_computation.2 | async-start | bytes 131072 | tf_op jit(solution)/shard_map/all_to_all | solution.py:100
  212.8 3.6 %all-to-all-done.1 = f32[4,1,4096]{2,1,0:T(1,128)S(1)} async-done(((f32[4,1,4096]{2,1,0:T(1,128)}), f32[4,1,4096]{2,1,0:T(1,128)S(1)}, u32[]{:S(2)}, u32[]{:S(2)}) %all-to-all-start.1) | async-done | bytes 65568 | tf_op jit(solution)/shard_map/all_to_all | solution.py:100
  216.3 0.9 reduce.1
  217.6 1.3 fusion.14
  218.9 1.3 fusion.16
  (75 shorter events, 16.9 us)
Async XLA Ops:
  7.2 5.9 %copy-start.3 = (f32[8]{0:T(128)S(1)}, f32[8]{0:T(128)}, u32[]{:S(2)}) copy-start(f32[8]{0:T(128)} %constant.153.clone) | copy-start | bytes 100
  7.2 5.9 %copy-start.4 = (f32[8]{0:T(128)S(1)}, f32[8]{0:T(128)}, u32[]{:S(2)}) copy-start(f32[8]{0:T(128)} %constant.154.clone) | copy-start | bytes 100
  7.2 159.2 %reduce-scatter.2.cloned.1.call-start = ((), (), s32[]{:S(2)}) async-start(), calls=%async_computation.3 | async-start | bytes 2162688 | tf_op jit(solution)/shard_map/reduce_scatter | solution.py:69
  13.8 4.3 %copy-start.5 = (s32[4]{0:T(128)S(1)}, s32[4]{0:T(128)}, u32[]{:S(2)}) copy-start(s32[4]{0:T(128)} %constant.155.clone) | copy-start | bytes 52
  13.8 4.3 %copy-start.6 = (s32[4]{0:T(128)S(1)}, s32[4]{0:T(128)}, u32[]{:S(2)}) copy-start(s32[4]{0:T(128)} %constant.156.clone) | copy-start | bytes 52
  22.8 1.0 copy-start.1
  23.9 52.5 %copy-start.2 = (s32[2,8,256]{2,1,0:T(8,128)S(1)}, s32[2,8,256]{2,1,0:T(8,128)}, u32[]{:S(2)}) copy-start(s32[2,8,256]{2,1,0:T(8,128)} %param.29) | copy-start | bytes 49156
  24.0 1.4 copy-start
  173.0 31.4 %all-to-all-start = ((f32[8,1,2048]{2,1,0:T(1,128)}), f32[8,1,2048]{2,1,0:T(1,128)S(1)}, u32[]{:S(2)}, u32[]{:S(2)}) async-start(f32[8,1,2048]{2,1,0:T(1,128)} %reshape.771), calls=%async_computation.1 | async-start | bytes 131072 | tf_op jit(solution)/shard_map/all_to_all | solution.py:101
  209.0 7.4 %all-to-all-start.1 = ((f32[4,1,4096]{2,1,0:T(1,128)}), f32[4,1,4096]{2,1,0:T(1,128)S(1)}, u32[]{:S(2)}, u32[]{:S(2)}) async-start(f32[4,1,4096]{2,1,0:T(1,128)} %reshape.773), calls=%async_computation.2 | async-start | bytes 131072 | tf_op jit(solution)/shard_map/all_to_all | solution.py:100
Sparse Core Ops, SparseCore 0:
  25.5 140.9 reduce-scatter.1

commit v2 on v0

--- a/solution.py
+++ b/solution.py
@@ -97,12 +97,20 @@
     middle = jnp.stack(
         [middle_cos[:, 0] - middle_sin[:, 1], middle_sin[:, 0] + middle_cos[:, 1]], axis=1
     )
-    arrived = lax.all_to_all(
-        lax.all_to_all(middle, "px", split_axis=3, concat_axis=4, tiled=True),
-        "py",
-        split_axis=3,
-        concat_axis=4,
-        tiled=True,
+    arrived = jnp.concatenate(
+        lax.all_to_all(
+            jnp.stack(
+                jnp.split(
+                    lax.all_to_all(middle, "px", split_axis=3, concat_axis=4, tiled=True),
+                    lax.axis_size("py"),
+                    axis=3,
+                )
+            ),
+            "py",
+            0,
+            0,
+        ),
+        axis=4,
     )
     x_slot = spectral // own_rows
     x_source = (x_slot % n_rows * n_columns + x_slot // n_rows) * own_rows + spectral % own_rows

time: 241 us -> 241 us (level)
  no operation moved by 1% of the time
where the time goes in v2:
time: 241 us
  waiting for transfers between devices  93.4 us (39%)
  blocking collectives  81.9 us (34%)
  other arithmetic  18.1 us (8%)
  between operations  16.4 us (7%)
  matrix products  12.8 us (5%)
  local copies, waits for them, and re-layouts  11.2 us (5%)
  starting transfers between devices  6.93 us (3%)
    reduce_scatter x1, waiting for transfers between devices, shards(): lax.psum_scatter(totals, ('px', 'py'), scatter_dimension=3, tiled=True)  89.8 us
    psum x1, blocking collectives, shards(): class_totals = lax.psum(local_counts, ('px', 'py'))  42 us
    psum x1, blocking collectives, shards(): shell_total = lax.psum(shell_part, ('px', 'py'))  39.9 us
    unnamed x22, local copies, waits for them, and re-layouts  7 us
    mul x7, other arithmetic, coverage(): spectral_abs[None, :] * rise_value  6 us
  transfers between devices with their start and end apart: 3, of which 2 were waited for; matrix products, arithmetic and copies ran while one was open for 4% of the time, Pallas kernels for 0%

profile of v2, /device:TPU:0, one launch (start us, length us, event | category | flops | bytes accessed | tf_op | source)
XLA Modules:
  0.0 240.6 jit_solution(2238187178344235930)
XLA Ops:
  7.9 1.1 copy.54
  9.0 2.0 fusion.38
  11.0 2.0 fusion.42
  14.5 1.5 convolution_bitcast_fusion.1
  16.0 1.5 convolution_bitcast_fusion
  18.1 0.8 fusion.81
  21.2 1.6 fusion.4
  23.0 0.9 copy-done.1
  24.0 1.3 copy-done
  25.6 42.0 %psum.14 = f32[2,4,2]{1,0,2:T(2,128)S(1)} all-reduce(f32[2,4,2]{1,0,2:T(2,128)S(1)} %multiply_bitcast_fusion), channel_id=1, replica_groups=mesh['px'=8,'py'=4] {'px','py'}, use_global_device_ids=true, to_apply=%region_5.6 | all-reduce | flops 16 | bytes 128 | tf_op jit(solution)/shard_map/psum | solution.py:74
  70.9 1.9 broadcast_multiply_fusion.10
  76.5 89.8 %reduce-scatter.2.cloned.1.call-done = f32[2,2,2,8,256]{4,3,2,1,0:T(8,128)} async-done(((f32[2,2,2,256,256]{4,3,2,1,0:T(8,128)}), f32[2,2,2,8,256]{4,3,2,1,0:T(8,128)}) %reduce-scatter.2.cloned.1.call-update) | async-done | bytes 65552 | tf_op jit(solution)/shard_map/reduce_scatter | solution.py:69
  166.3 0.8 broadcast_divide_fusion
  167.2 1.3 convolution_bitcast_fusion.2
  168.5 1.3 convolution_bitcast_fusion.3
  170.6 2.2 reshape.779
  172.9 3.4 %all-to-all-start = ((f32[8,1,2048]{2,1,0:T(1,128)}), f32[8,1,2048]{2,1,0:T(1,128)S(1)}, u32[]{:S(2)}, u32[]{:S(2)}) async-start(f32[8,1,2048]{2,1,0:T(1,128)} %reshape.779), calls=%async_computation.1 | async-start | bytes 131072 | tf_op jit(solution)/shard_map/all_to_all | solution.py:104
  176.6 39.9 %psum.15 = f32[3,32]{1,0:T(4,128)S(1)} all-reduce(f32[3,32]{1,0:T(4,128)S(1)} %fusion.5), channel_id=1, replica_groups=mesh['px'=8,'py'=4] {'px','py'}, use_global_device_ids=true, to_apply=%region_22.23 | all-reduce | flops 96 | bytes 768 | tf_op jit(solution)/shard_map/psum | solution.py:90
  217.9 1.6 reshape.780
  221.6 3.5 %all-to-all-start.1 = ((f32[4,1,4096]{2,1,0:T(1,128)}), f32[4,1,4096]{2,1,0:T(1,128)S(1)}, u32[]{:S(2)}, u32[]{:S(2)}) async-start(f32[4,1,4096]{2,1,0:T(1,128)} %reshape.781), calls=%async_computation.2 | async-start | bytes 131072 | tf_op jit(solution)/shard_map/all_to_all | solution.py:101
  225.7 3.6 %all-to-all-done.1 = f32[4,1,4096]{2,1,0:T(1,128)S(1)} async-done(((f32[4,1,4096]{2,1,0:T(1,128)}), f32[4,1,4096]{2,1,0:T(1,128)S(1)}, u32[]{:S(2)}, u32[]{:S(2)}) %all-to-all-start.1) | async-done | bytes 65568 | tf_op jit(solution)/shard_map/all_to_all | solution.py:101
  229.3 0.9 reduce.1
  230.5 1.3 fusion.14
  231.8 1.3 fusion.16
  (78 shorter events, 16.7 us)
Async XLA Ops:
  7.2 5.9 %copy-start.3 = (f32[8]{0:T(128)S(1)}, f32[8]{0:T(128)}, u32[]{:S(2)}) copy-start(f32[8]{0:T(128)} %constant.153.clone) | copy-start | bytes 100
  7.2 5.9 %copy-start.4 = (f32[8]{0:T(128)S(1)}, f32[8]{0:T(128)}, u32[]{:S(2)}) copy-start(f32[8]{0:T(128)} %constant.154.clone) | copy-start | bytes 100
  7.2 159.1 %reduce-scatter.2.cloned.1.call-start = ((), (), s32[]{:S(2)}) async-start(), calls=%async_computation.3 | async-start | bytes 2162688 | tf_op jit(solution)/shard_map/reduce_scatter | solution.py:69
  13.8 4.3 %copy-start.5 = (s32[4]{0:T(128)S(1)}, s32[4]{0:T(128)}, u32[]{:S(2)}) copy-start(s32[4]{0:T(128)} %constant.155.clone) | copy-start | bytes 52
  13.8 4.3 %copy-start.6 = (s32[4]{0:T(128)S(1)}, s32[4]{0:T(128)}, u32[]{:S(2)}) copy-start(s32[4]{0:T(128)} %constant.156.clone) | copy-start | bytes 52
  22.8 1.0 copy-start.1
  23.9 52.5 %copy-start.2 = (s32[2,8,256]{2,1,0:T(8,128)S(1)}, s32[2,8,256]{2,1,0:T(8,128)}, u32[]{:S(2)}) copy-start(s32[2,8,256]{2,1,0:T(8,128)} %param.29) | copy-start | bytes 49156
  24.0 1.4 copy-start
  172.9 43.6 %all-to-all-start = ((f32[8,1,2048]{2,1,0:T(1,128)}), f32[8,1,2048]{2,1,0:T(1,128)S(1)}, u32[]{:S(2)}, u32[]{:S(2)}) async-start(f32[8,1,2048]{2,1,0:T(1,128)} %reshape.779), calls=%async_computation.1 | async-start | bytes 131072 | tf_op jit(solution)/shard_map/all_to_all | solution.py:104
  221.6 7.7 %all-to-all-start.1 = ((f32[4,1,4096]{2,1,0:T(1,128)}), f32[4,1,4096]{2,1,0:T(1,128)S(1)}, u32[]{:S(2)}, u32[]{:S(2)}) async-start(f32[4,1,4096]{2,1,0:T(1,128)} %reshape.781), calls=%async_computation.2 | async-start | bytes 131072 | tf_op jit(solution)/shard_map/all_to_all | solution.py:101
Sparse Core Ops, SparseCore 0:
  25.5 140.7 reduce-scatter.1
